TPU v7x, 32 devices: a whole 2x2x4 slice. The times are simulated.
32 devices in a mesh: dp: 8 (over z, y), seq: 4 (over x, core).
Axes of the slice: x: 2, y: 2, z: 4, core: 2. Of those that a mesh axis runs over, the one named last changes fastest.
Arguments:
- tokens: bfloat16 [16384, 1024], P(('dp', 'seq')), may hold values from -6 to 6
- doc_starts: int32 [8, 4], P('dp'), may hold values from 0 to 2047, as said below
- routes: int32 [16384, 1], P(('dp', 'seq')), may hold values from 0 to 63; in each aligned block of 512 rows (0 to 511, 512 to 1023, ...) at most 16 rows name the same one
- ln1_gain: bfloat16 [1024], P('seq'), may hold values from 0.5 to 1.5
- ln1_bias: bfloat16 [1024], P('seq'), may hold values from -4 to 4
- w_qkv: bfloat16 [1024, 3072], P('seq'), may hold values from -0.1875 to 0.1875
- w_proj: bfloat16 [1024, 1024], P('seq'), may hold values from -0.75 to 0.75
- ln2_gain: bfloat16 [1024], P('seq'), may hold values from 0.5 to 1.5
- ln2_bias: bfloat16 [1024], P('seq'), may hold values from -4 to 4
- w_router: bfloat16 [1024, 64], P('seq'), may hold values from -0.09375 to 0.09375
- w_expert_in: bfloat16 [64, 1024, 4096], P('dp', None, 'seq'), may hold values from -0.1875 to 0.1875
- w_expert_out: bfloat16 [64, 4096, 1024], P('dp', 'seq'), may hold values from -12 to 12
- out_grad: bfloat16 [16384, 1024], P(('dp', 'seq')), may hold values from -6 to 6
Outputs:
- output: bfloat16 [16384, 1024], P(('dp', 'seq'))
- input_grad: float32 [16384, 1024], P(('dp', 'seq'))
- ln1_gain_grad: float32 [1024], P('seq')
- ln1_bias_grad: float32 [1024], P('seq')
- w_qkv_grad: float32 [1024, 3072], P('seq')
- w_proj_grad: float32 [1024, 1024], P('seq')
- ln2_gain_grad: float32 [1024], P('seq')
- ln2_bias_grad: float32 [1024], P('seq')
- w_router_grad: float32 [1024, 64], P('seq')
- w_expert_in_grad: float32 [64, 1024, 4096], P('dp', None, 'seq')
- w_expert_out_grad: float32 [64, 4096, 1024], P('dp', 'seq')
Inputs may be any that keep to these rules, and one draw needn't show every extreme that they name: `doc_starts`: each row begins with 0 and rises strictly; entry j is where document j of sequence r begins. `routes`: among the 512 rows of one device (aligned blocks), no expert is named more than 16 times, a bound that some block reaches.
All inputs are finite; a program needn't handle non-finite values.
Results may differ from a plain program's by a relative error of at most 0.02.
Values may be sent and summed in bfloat16 or wider, within the bound.
A program may use at most 320 MiB of HBM per device.

v0:
```python
import jax
import jax.numpy as jnp
from jax import lax
from jax.sharding import PartitionSpec as P

H = 16
HD = 64
EXPERTS = 64
TOK_DEV = 512


EPS = 1e-05
NEG = -1e30


def normalize(values):
    center = values - jnp.mean(values, axis=-1, keepdims=True)
    inverse = lax.rsqrt(jnp.mean(center * center, axis=-1, keepdims=True) + EPS)
    return (center * inverse, inverse)


def norm_back(grad_norm, normed, inverse):
    first_mean = jnp.mean(grad_norm, axis=-1, keepdims=True)
    second_mean = jnp.mean(grad_norm * normed, axis=-1, keepdims=True)
    return inverse * (grad_norm - first_mean - normed * second_mean)


def collect_rows(rows_part, grads_part):
    return (
        lax.all_gather(rows_part, "seq", axis=1, tiled=True),
        lax.all_gather(grads_part, "seq", axis=1, tiled=True),
    )


def route_rows(rows_part, grads_part):
    return (
        lax.all_to_all(rows_part, "dp", split_axis=0, concat_axis=0, tiled=True),
        lax.all_to_all(grads_part, "dp", split_axis=0, concat_axis=0, tiled=True),
    )


def expert_work(rows_in, grads_in, first_weight, second_weight):
    pre_act = jnp.einsum(
        "abecd,edf->abecf", rows_in, first_weight, preferred_element_type=jnp.float32
    )
    hidden_exp, gelu_back = jax.vjp(jax.nn.gelu, pre_act)
    hidden_low = hidden_exp.astype(jnp.bfloat16)
    part_out = jnp.einsum(
        "abecf,efd->abecd", hidden_low, second_weight, preferred_element_type=jnp.float32
    )
    grad_hidden = jnp.einsum(
        "abecd,efd->abecf", grads_in, second_weight, preferred_element_type=jnp.float32
    )
    grad_pre = gelu_back(grad_hidden)[0].astype(jnp.bfloat16)
    first_grad = jnp.einsum(
        "abecd,abecf->edf", rows_in, grad_pre, preferred_element_type=jnp.float32
    )
    second_grad = jnp.einsum(
        "abecf,abecd->efd", hidden_low, grads_in, preferred_element_type=jnp.float32
    )
    part_dx = jnp.einsum(
        "abecf,edf->abecd", grad_pre, first_weight, preferred_element_type=jnp.float32
    )
    return (part_out, part_dx, first_grad, second_grad)


def per_device(
    tokens,
    doc_starts,
    routes,
    ln1_gain,
    ln1_bias,
    w_qkv,
    w_proj,
    ln2_gain,
    ln2_bias,
    w_router,
    w_expert_in,
    w_expert_out,
    out_grad,
):
    seq_count = lax.axis_size("seq")
    dp_count = lax.axis_size("dp")
    gathered_weights = (
        lax.all_gather(w_qkv, "seq", axis=0, tiled=True),
        lax.all_gather(w_proj, "seq", axis=0, tiled=True),
        lax.all_gather(w_router, "seq", axis=0, tiled=True),
        lax.all_gather(ln1_gain, "seq", axis=0, tiled=True),
        lax.all_gather(ln1_bias, "seq", axis=0, tiled=True),
        lax.all_gather(ln2_gain, "seq", axis=0, tiled=True),
        lax.all_gather(ln2_bias, "seq", axis=0, tiled=True),
    )
    qkv_weight = gathered_weights[0]
    proj_weight = gathered_weights[1]
    router_weight = gathered_weights[2]
    gain_one = gathered_weights[3].astype(jnp.float32)
    bias_one = gathered_weights[4].astype(jnp.float32)
    gain_two = gathered_weights[5].astype(jnp.float32)
    bias_two = gathered_weights[6].astype(jnp.float32)
    inputs = tokens.astype(jnp.float32)
    row_count = inputs.shape[0]
    width = inputs.shape[1]
    normed_one, inverse_one = normalize(inputs)
    hidden_one = (normed_one * gain_one + bias_one).astype(jnp.bfloat16)
    qkv_local = jnp.dot(hidden_one, qkv_weight, preferred_element_type=jnp.float32).astype(
        jnp.bfloat16
    )
    heads_here = H // seq_count
    head_width = heads_here * HD
    length = row_count * seq_count
    qkv_heads = lax.all_to_all(
        qkv_local.reshape(row_count, 3, seq_count, head_width),
        "seq",
        split_axis=2,
        concat_axis=0,
        tiled=True,
    )
    queries = qkv_heads[:, 0, 0].reshape(length, heads_here, HD)
    key_rows = qkv_heads[:, 1, 0].reshape(length, heads_here, HD)
    value_rows = qkv_heads[:, 2, 0].reshape(length, heads_here, HD)
    starts = doc_starts[0]
    positions = jnp.arange(length, dtype=jnp.int32)
    doc_first = jnp.max(
        jnp.where(starts[None, :] <= positions[:, None], starts[None, :], 0), axis=1
    )
    block_rows = min(512, length)
    block_count = length // block_rows
    factor = HD ** (-0.5)

    def block_scores(block_index):
        begin = block_index * block_rows
        query_block = lax.dynamic_slice_in_dim(queries, begin, block_rows, 0)
        first_block = lax.dynamic_slice_in_dim(doc_first, begin, block_rows, 0)
        query_pos = begin + jnp.arange(block_rows, dtype=jnp.int32)
        allowed = (positions[None, :] <= query_pos[:, None]) & (
            positions[None, :] >= first_block[:, None]
        )
        scores = (
            jnp.einsum("qhd,khd->hqk", query_block, key_rows, preferred_element_type=jnp.float32)
            * factor
        )
        return jnp.where(allowed[None], scores, NEG)

    def forward_block(block_index):
        scores = block_scores(block_index)
        row_top = jnp.max(scores, axis=-1, keepdims=True)
        weights = jnp.exp(scores - row_top)
        totals = jnp.sum(weights, axis=-1, keepdims=True)
        probs_low = (weights / totals).astype(jnp.bfloat16)
        attended = jnp.einsum(
            "hqk,khd->qhd", probs_low, value_rows, preferred_element_type=jnp.float32
        ).astype(jnp.bfloat16)
        return (attended, (row_top + jnp.log(totals))[:, :, 0])

    attended_all, log_totals = lax.map(forward_block, jnp.arange(block_count, dtype=jnp.int32))
    heads_out = attended_all.reshape(length, head_width)
    token_heads = lax.all_to_all(heads_out, "seq", split_axis=0, concat_axis=1, tiled=True)
    middle = inputs + jnp.dot(token_heads, proj_weight, preferred_element_type=jnp.float32)
    normed_two, inverse_two = normalize(middle)
    hidden_two = (normed_two * gain_two + bias_two).astype(jnp.bfloat16)
    logits = jnp.dot(hidden_two, router_weight, preferred_element_type=jnp.float32)
    logit_top = jnp.max(logits, axis=-1, keepdims=True)
    logit_exp = jnp.exp(logits - logit_top)
    probs = logit_exp / jnp.sum(logit_exp, axis=-1, keepdims=True)
    expert_ids = routes[:, 0]
    expert_range = jnp.arange(EXPERTS, dtype=jnp.int32)
    selector = expert_ids[:, None] == expert_range[None, :]
    selector_float = selector.astype(jnp.float32)
    gate = jnp.sum(probs * selector_float, axis=1)
    capacity = max(2, 2 * TOK_DEV // EXPERTS)
    onehot_int = selector.astype(jnp.int32)
    ranking = jnp.sum((jnp.cumsum(onehot_int, axis=0) - 1) * onehot_int, axis=1)
    slot_ids = expert_ids * capacity + ranking
    placement_map = (
        jnp.arange(EXPERTS * capacity, dtype=jnp.int32)[:, None] == slot_ids[None, :]
    ).astype(jnp.bfloat16)
    grad_out = out_grad.astype(jnp.float32)
    scaled_grad = (gate[:, None] * grad_out).astype(jnp.bfloat16)
    local_experts = EXPERTS // dp_count
    buffer_shape = (dp_count, 1, local_experts, capacity, width)
    send_rows = (
        jnp.dot(placement_map, hidden_two, preferred_element_type=jnp.float32)
        .astype(jnp.bfloat16)
        .reshape(buffer_shape)
    )
    send_grads = (
        jnp.dot(placement_map, scaled_grad, preferred_element_type=jnp.float32)
        .astype(jnp.bfloat16)
        .reshape(buffer_shape)
    )
    collected = collect_rows(send_rows, send_grads)
    arrived = route_rows(collected[0], collected[1])
    part_out, part_dx, expert_in_grad, expert_out_grad = expert_work(
        arrived[0], arrived[1], w_expert_in, w_expert_out
    )
    summed_rows = (
        lax.psum_scatter(
            part_out.astype(jnp.bfloat16), "seq", scatter_dimension=1, tiled=True
        ).astype(jnp.float32),
        lax.psum_scatter(
            part_dx.astype(jnp.bfloat16), "seq", scatter_dimension=1, tiled=True
        ).astype(jnp.float32),
    )
    rows_out = summed_rows[0]
    rows_dx = summed_rows[1]
    back_rows = (
        lax.all_to_all(
            rows_out.astype(jnp.bfloat16), "dp", split_axis=0, concat_axis=0, tiled=True
        ),
        lax.all_to_all(rows_dx.astype(jnp.bfloat16), "dp", split_axis=0, concat_axis=0, tiled=True),
    )
    flat_out = back_rows[0].reshape(EXPERTS * capacity, width)
    flat_dx = back_rows[1].reshape(EXPERTS * capacity, width)
    expert_out = jnp.einsum(
        "sr,sd->rd", placement_map, flat_out, preferred_element_type=jnp.float32
    )
    expert_dx = jnp.einsum("sr,sd->rd", placement_map, flat_dx, preferred_element_type=jnp.float32)
    output = (middle + gate[:, None] * expert_out).astype(jnp.bfloat16)
    grad_gate = jnp.sum(grad_out * expert_out, axis=1)
    grad_logits = probs * (selector_float - gate[:, None]) * grad_gate[:, None]
    router_grad = jnp.dot(
        hidden_two.astype(jnp.float32).T, grad_logits, precision=lax.Precision.HIGHEST
    )
    grad_two = expert_dx + jnp.dot(
        grad_logits, router_weight.astype(jnp.float32).T, precision=lax.Precision.HIGHEST
    )
    gain_two_grad = jnp.sum(grad_two * normed_two, axis=0)
    bias_two_grad = jnp.sum(grad_two, axis=0)
    grad_middle = grad_out + norm_back(grad_two * gain_two, normed_two, inverse_two)
    grad_branch = grad_middle.astype(jnp.bfloat16)
    proj_grad = jnp.dot(token_heads.T, grad_branch, preferred_element_type=jnp.float32)
    grad_heads_tok = jnp.dot(grad_branch, proj_weight.T, preferred_element_type=jnp.float32).astype(
        jnp.bfloat16
    )
    grad_heads = lax.all_to_all(grad_heads_tok, "seq", split_axis=1, concat_axis=0, tiled=True)
    grad_attended = grad_heads.reshape(length, heads_here, HD)

    def backward_block(carry, block_index):
        key_acc, value_acc = carry
        begin = block_index * block_rows
        query_block = lax.dynamic_slice_in_dim(queries, begin, block_rows, 0)
        grad_block = lax.dynamic_slice_in_dim(grad_attended, begin, block_rows, 0)
        scores = block_scores(block_index)
        probs_block = jnp.exp(scores - log_totals[block_index][:, :, None])
        grad_probs = jnp.einsum(
            "qhd,khd->hqk", grad_block, value_rows, preferred_element_type=jnp.float32
        )
        row_dot = jnp.sum(probs_block * grad_probs, axis=-1, keepdims=True)
        grad_scores = (probs_block * (grad_probs - row_dot)).astype(jnp.bfloat16)
        grad_query = (
            jnp.einsum("hqk,khd->qhd", grad_scores, key_rows, preferred_element_type=jnp.float32)
            * factor
        ).astype(jnp.bfloat16)
        key_acc = (
            key_acc
            + jnp.einsum(
                "hqk,qhd->khd", grad_scores, query_block, preferred_element_type=jnp.float32
            )
            * factor
        )
        value_acc = value_acc + jnp.einsum(
            "hqk,qhd->khd",
            probs_block.astype(jnp.bfloat16),
            grad_block,
            preferred_element_type=jnp.float32,
        )
        return ((key_acc, value_acc), grad_query)

    zero_rows = jnp.zeros((length, heads_here, HD), jnp.float32)
    carried, query_grad = lax.scan(
        backward_block, (zero_rows, zero_rows), jnp.arange(block_count, dtype=jnp.int32)
    )
    grad_qkv_heads = jnp.stack(
        [
            query_grad.reshape(length, head_width),
            carried[0].astype(jnp.bfloat16).reshape(length, head_width),
            carried[1].astype(jnp.bfloat16).reshape(length, head_width),
        ],
        axis=1,
    )[:, :, None, :]
    grad_qkv = lax.all_to_all(
        grad_qkv_heads, "seq", split_axis=0, concat_axis=2, tiled=True
    ).reshape(row_count, 3 * width)
    qkv_grad = jnp.dot(hidden_one.T, grad_qkv, preferred_element_type=jnp.float32)
    grad_one = jnp.dot(grad_qkv, qkv_weight.T, preferred_element_type=jnp.float32)
    gain_one_grad = jnp.sum(grad_one * normed_one, axis=0)
    bias_one_grad = jnp.sum(grad_one, axis=0)
    input_grad = grad_middle + norm_back(grad_one * gain_one, normed_one, inverse_one)
    summed = (
        lax.psum_scatter(
            qkv_grad.astype(jnp.bfloat16), "seq", scatter_dimension=0, tiled=True
        ).astype(jnp.float32),
        lax.psum_scatter(
            proj_grad.astype(jnp.bfloat16), "seq", scatter_dimension=0, tiled=True
        ).astype(jnp.float32),
        lax.psum_scatter(
            router_grad.astype(jnp.bfloat16), "seq", scatter_dimension=0, tiled=True
        ).astype(jnp.float32),
        lax.psum_scatter(
            gain_one_grad.astype(jnp.bfloat16), "seq", scatter_dimension=0, tiled=True
        ).astype(jnp.float32),
        lax.psum_scatter(
            bias_one_grad.astype(jnp.bfloat16), "seq", scatter_dimension=0, tiled=True
        ).astype(jnp.float32),
        lax.psum_scatter(
            gain_two_grad.astype(jnp.bfloat16), "seq", scatter_dimension=0, tiled=True
        ).astype(jnp.float32),
        lax.psum_scatter(
            bias_two_grad.astype(jnp.bfloat16), "seq", scatter_dimension=0, tiled=True
        ).astype(jnp.float32),
    )
    reduced = (
        lax.psum(summed[0].astype(jnp.bfloat16), "dp").astype(jnp.float32),
        lax.psum(summed[1].astype(jnp.bfloat16), "dp").astype(jnp.float32),
        lax.psum(summed[2].astype(jnp.bfloat16), "dp").astype(jnp.float32),
        lax.psum(summed[3].astype(jnp.bfloat16), "dp").astype(jnp.float32),
        lax.psum(summed[4].astype(jnp.bfloat16), "dp").astype(jnp.float32),
        lax.psum(summed[5].astype(jnp.bfloat16), "dp").astype(jnp.float32),
        lax.psum(summed[6].astype(jnp.bfloat16), "dp").astype(jnp.float32),
    )
    return (
        output,
        input_grad,
        reduced[3],
        reduced[4],
        reduced[0],
        reduced[1],
        reduced[5],
        reduced[6],
        reduced[2],
        expert_in_grad,
        expert_out_grad,
    )


def solution(mesh):
    in_specs = (
        P(("dp", "seq"), None),
        P("dp", None),
        P(("dp", "seq"), None),
        P("seq"),
        P("seq"),
        P("seq", None),
        P("seq", None),
        P("seq"),
        P("seq"),
        P("seq", None),
        P("dp", None, "seq"),
        P("dp", "seq", None),
        P(("dp", "seq"), None),
    )
    out_specs = (
        P(("dp", "seq"), None),
        P(("dp", "seq"), None),
        P("seq"),
        P("seq"),
        P("seq", None),
        P("seq", None),
        P("seq"),
        P("seq"),
        P("seq", None),
        P("dp", None, "seq"),
        P("dp", "seq", None),
    )
    return jax.shard_map(
        per_device, mesh=mesh, in_specs=in_specs, out_specs=out_specs, check_vma=False
    )
```

profile of v0, /device:TPU:0, one launch (start us, length us, event | category | flops | bytes accessed | tf_op | source)
XLA Modules:
  0.0 1635.8 jit_solution(8930138773344012550)
XLA Ops:
  9.2 6.0 all-gather.1
  24.0 34.7 %all-gather.9.cloned.1.call-done = bf16[1024,3072]{1,0:T(8,128)(2,1)} async-done(((bf16[256,3072]{1,0:T(8,128)(2,1)}), bf16[1024,3072]{1,0:T(8,128)(2,1)}) %all-gather.9.cloned.1.call-update) | async-done | bytes 6291472 | tf_op jit(solution)/shard_map/all_gather | solution.py:85
  58.7 8.3 convolution_convert_fusion.1
  79.4 47.3 %all-to-all-done = bf16[512,3,4,256]{3,0,1,2:T(8,128)(2,1)S(1)} async-done(((bf16[512,3,4,256]{3,0,1,2:T(8,128)(2,1)}), bf16[512,3,4,256]{3,0,1,2:T(8,128)(2,1)S(1)}, u32[]{:S(2)}, u32[]{:S(2)}) %all-to-all-start) | async-done | bytes 3145760 | tf_op jit(solution)/shard_map/all_to_all | solution.py:111
  131.9 67.1 %while.30 = (s32[]{:T(128)}, bf16[4,512,4,64]{1,3,2,0:T(8,128)(2,1)}, f32[4,4,512]{2,1,0:T(4,128)}, s32[4]{0:T(128)S(1)}, s32[2048]{0:T(1024)S(1)}, /*index=5*/b...) while((s32[]{:T(128)}, ...), condition=%wide.region_6.7_spmd.clone.clone, body=%wide.region_3.6_spmd.clone.clone.sunk | while | flops 1127348736 | bytes 57223368 | solution.py:155
  142.1 5.9 fusion.172
  158.9 5.9 fusion.172
  175.7 5.9 fusion.172
  192.4 5.9 fusion.172
  203.3 15.3 all-gather.3
  232.6 58.4 %all-gather.13.cloned.1.call-done = bf16[8,4,8,16,1024]{4,3,1,2,0:T(8,128)(2,1)} async-done(((bf16[8,1,8,16,1024]{4,3,1,2,0:T(8,128)(2,1)}), bf16[8,4,8,16,1024]{4,3,1,2,0:T(8,128)(2,1)}) %all-gather.13.cloned.1.call-update) | async-done | bytes 8388624 | tf_op jit(solution)/shard_map/all_gather | solution.py:30
  307.7 58.9 %all-gather.15.cloned.1.call-done = bf16[8,4,8,16,1024]{4,3,1,2,0:T(8,128)(2,1)} async-done(((bf16[8,1,8,16,1024]{4,3,1,2,0:T(8,128)(2,1)}), bf16[8,4,8,16,1024]{4,3,1,2,0:T(8,128)(2,1)}) %all-gather.15.cloned.1.call-update) | async-done | bytes 8388624 | tf_op jit(solution)/shard_map/all_gather | solution.py:31
  366.7 113.5 %all-to-all-done.2 = bf16[8,4,8,16,1024]{4,3,1,2,0:T(8,128)(2,1)} async-done(((bf16[8,4,8,16,1024]{4,3,1,2,0:T(8,128)(2,1)}), bf16[8,4,8,16,1024]{4,3,1,2,0:T(8,128)(2,1)}, u32[]{:S(2)}, u32[]{:S(2)}) %all-to-all-start.2) | async-done | bytes 8388640 | tf_op jit(solution)/shard_map/all_to_all | solution.py:37
  485.6 24.4 %fusion.62 = (bf16[8,4,8,16,1024]{4,3,1,0,2:T(8,128)(2,1)}, f32[8,8,4,16,1024]{4,3,2,1,0:T(8,128)}) fusion(bf16[8,1024,1024]{2,1,0:T(8,128)(2,1)} %param.27, bf16[8,4,8,16,1024]{4,3,1,2,0:T(8,128)(2,1)} %all-to-all-done.2), kind=kOutput, calls=%fused_computation.76 | convolution fusion | flops 8627683328 | bytes 50331648 | tf_op jit(solution)/shard_map/abecd,edf->abecf/dot_general | solution.py:43
  510.0 157.7 %all-to-all-done.4 = bf16[8,4,8,16,1024]{4,3,1,2,0:T(8,128)(2,1)} async-done(((bf16[8,4,8,16,1024]{4,3,1,2,0:T(8,128)(2,1)}), bf16[8,4,8,16,1024]{4,3,1,2,0:T(8,128)(2,1)}, u32[]{:S(2)}, u32[]{:S(2)}) %all-to-all-start.4) | async-done | bytes 8388640 | tf_op jit(solution)/shard_map/all_to_all | solution.py:38
  667.7 25.7 %fusion.50 = bf16[8,4,8,16,1024]{4,3,1,0,2:T(8,128)(2,1)} fusion(f32[8,8,4,16,1024]{4,3,2,1,0:T(8,128)} %get-tuple-element.341, bf16[8,1024,1024]{2,1,0:T(8,128)(2,1)} %param.28, bf16[8,4,8,16,1024]{4,3,1,2,0:T(8,128)(2,1)} %all-to-all-done.4), kind=kOutput, calls=%fused_computation.61 | convolution fusion | flops 8673820672 | bytes 50331648 | tf_op jit(solution)/shard_map/abecd,efd->abecf/dot_general | solution.py:51
  693.4 15.8 convert_bitcast_fusion
  709.3 18.1 %convert_bitcast_fusion.1 = bf16[8,4,8,16,1024]{4,3,1,0,2:T(8,128)(2,1)} fusion(bf16[8,4,8,16,1024]{4,3,1,0,2:T(8,128)(2,1)} %get-tuple-element.340, bf16[8,1024,1024]{2,1,0:T(8,128)(2,1)} %param.28), kind=kOutput, calls=%fused_computation.84 | convolution fusion | flops 8594128896 | bytes 33554432 | tf_op jit(solution)/shard_map/abecf,efd->abecd/dot_general | solution.py:48
  728.6 285.9 %all-reduce.15.cloned.1.call-done = (bf16[8,4,8,16,1024]{4,3,1,0,2:T(8,128)(2,1)}, bf16[8,4,8,16,1024]{4,3,1,0,2:T(8,128)(2,1)}) async-done(((bf16[8,4,8,16,1024]{4,3,1,0,2:T(8,128)(2,1)}, bf16[8,4,8,16,1024]{4,3,1,0,2:T(8,128)(2,1)}), (bf16[8,4,8,16,1024]{4,3,1,0,2:T(8,128)(2,1)}, bf16[8,4,8,16,1024]{4,3,1,0,2:T(8,128)(2,1)})) %all-reduce.15.cloned.1.call-update) | async-done | bytes 16777232
  1027.9 44.4 %all-to-all-done.3 = bf16[8,1,8,16,1024]{4,3,1,2,0:T(8,128)(2,1)} async-done(((bf16[8,1,8,16,1024]{4,3,1,2,0:T(8,128)(2,1)}), bf16[8,1,8,16,1024]{4,3,1,2,0:T(8,128)(2,1)}, u32[]{:S(2)}, u32[]{:S(2)}) %all-to-all-start.3) | async-done | bytes 2097184 | tf_op jit(solution)/shard_map/all_to_all | solution.py:207
  1081.3 43.3 %all-to-all-done.5 = bf16[8,1,8,16,1024]{4,3,1,2,0:T(8,128)(2,1)} async-done(((bf16[8,1,8,16,1024]{4,3,1,2,0:T(8,128)(2,1)}), bf16[8,1,8,16,1024]{4,3,1,2,0:T(8,128)(2,1)}, u32[]{:S(2)}, u32[]{:S(2)}) %all-to-all-start.5) | async-done | bytes 2097184 | tf_op jit(solution)/shard_map/all_to_all | solution.py:210
  1142.5 9.8 all-to-all-done.6
  1156.1 203.3 %while.31 = (s32[]{:T(128)}, f32[2048,4,64]{0,2,1:T(8,128)}, f32[2048,4,64]{0,2,1:T(8,128)}, bf16[4,512,4,64]{1,3,2,0:T(8,128)(2,1)}, s32[4]{0:T(128)S(1)}, /*in...) while((s32[]{:T(128)}, f32[2048,4,64]{0,2,1:T(8,128)}, ...), condition=%wide.region_22.23_spmd.clone.clone, body=%wide.region_20.22_spmd.clone.clone.sunk | while | flops 2753296896 | bytes 184945072 | solution.py:270
  1165.6 7.2 fusion.185
  1172.8 11.6 multiply_reduce_fusion.7
  1184.4 10.9 multiply_convert_fusion.2
  1195.3 7.1 fusion.186
  1215.5 7.6 fusion.185
  1223.1 11.5 multiply_reduce_fusion.7
  1234.6 10.9 multiply_convert_fusion.2
  1245.5 7.1 fusion.186
  1266.4 7.6 fusion.185
  1274.0 11.5 multiply_reduce_fusion.7
  1285.6 10.9 multiply_convert_fusion.2
  1296.4 7.1 fusion.186
  1317.4 7.6 fusion.185
  1325.0 11.5 multiply_reduce_fusion.7
  1336.5 10.9 multiply_convert_fusion.2
  1347.4 7.1 fusion.186
  1370.3 51.9 %all_to_all.88 = bf16[2048,3,1,256]{3,1,2,0:T(4,128)(2,1)S(1)} all-to-all(bf16[2048,3,1,256]{3,1,2,0:T(4,128)(2,1)} %copy.112), channel_id=1, replica_groups=mesh['dp'=8,'seq'=4] {'seq'}, dimensions={0} | all-to-all | bytes 6291456 | tf_op jit(solution)/shard_map/all_to_all | solution.py:281
  1429.1 7.8 convolution_convert_fusion
  1439.6 23.5 %convolution_bitcast_fusion = f32[8,1024,1024]{2,1,0:T(8,128)} fusion(bf16[8,4,8,16,1024]{4,3,1,2,0:T(8,128)(2,1)} %all-to-all-done.4, bf16[8,4,8,16,1024]{4,3,1,0,2:T(8,128)(2,1)} %get-tuple-element.340), kind=kOutput, calls=%fused_computation.77 | convolution fusion | flops 8589934592 | bytes 50331648 | tf_op jit(solution)/shard_map/abecf,abecd->efd/dot_general | solution.py:58
  1463.1 30.5 %reduce-scatter.10.cloned.1.call-done = bf16[256,3072]{1,0:T(8,128)(2,1)} async-done(((bf16[1024,3072]{1,0:T(8,128)(2,1)}), bf16[256,3072]{1,0:T(8,128)(2,1)}) %reduce-scatter.10.cloned.1.call-update) | async-done | bytes 1572880 | tf_op jit(solution)/shard_map/reduce_scatter | solution.py:290
  1493.6 20.0 %convolution_bitcast_fusion.1 = f32[8,1024,1024]{2,1,0:T(8,128)} fusion(bf16[8,4,8,16,1024]{4,3,1,2,0:T(8,128)(2,1)} %all-to-all-done.2, bf16[8,4,8,16,1024]{4,3,1,0,2:T(8,128)(2,1)} %fusion.50), kind=kOutput, calls=%fused_computation.78 | convolution fusion | flops 8589934592 | bytes 50331648 | tf_op jit(solution)/shard_map/abecd,abecf->edf/dot_general | solution.py:55
  1513.7 9.2 fusion.85
  1522.9 5.8 all-reduce.8
  1529.0 39.5 %all-reduce.6 = (bf16[256]{0:T(256)(128)(2,1)S(1)}, bf16[256]{0:T(256)(128)(2,1)S(1)}, bf16[256]{0:T(256)(128)(2,1)S(1)}, bf16[256]{0:T(256)(128)(2,1)S(1)}, bf16[256,64]{0,1:T(8,128)(2,1)S(1)}) all-reduce(bf16[256]{0:T(256)(128)(2,1)S(1)} %dynamic-slice.5, ...), channel_id=1, replica_groups=mesh['dp'=8,'seq'=4] {'dp'}, use_global_device_ids=true, to_apply=%region_27.28 | all-reduce | flops 17408 | bytes 69632 | tf_op jit(solution)/shard_map/psum | solution.py:316
  1575.0 48.4 %all-reduce.13.cloned.1.call-done = (bf16[256,3072]{1,0:T(8,128)(2,1)}, bf16[256,1024]{1,0:T(8,128)(2,1)}) async-done(((bf16[256,3072]{1,0:T(8,128)(2,1)}, bf16[256,1024]{1,0:T(8,128)(2,1)}), (bf16[256,3072]{1,0:T(8,128)(2,1)}, bf16[256,1024]{1,0:T(8,128)(2,1)})) %all-reduce.13.cloned.1.call-update) | async-done | bytes 2097168 | tf_op jit(solution)/shard_map/psum | solution.py:313
  (296 shorter events, 230.4 us)
Async XLA Ops:
  7.2 51.5 %all-gather.9.cloned.1.call-start = ((), (), s32[]{:S(2)}) async-start(), calls=%async_computation.11 | async-start | bytes 7864320 | tf_op jit(solution)/shard_map/all_gather | solution.py:85
  15.2 43.5 %copy-start.40 = (f32[4,1,256]{2,1,0:T(1,128)}, f32[4,1,256]{2,1,0:T(1,128)S(1)}, u32[]{:S(2)}) copy-start(f32[4,1,256]{2,1,0:T(1,128)S(1)} %convert_element_type.208) | copy-start | bytes 12292
  20.6 38.1 %copy-start.32 = (f32[4,1,256]{2,1,0:T(1,128)}, f32[4,1,256]{2,1,0:T(1,128)S(1)}, u32[]{:S(2)}) copy-start(f32[4,1,256]{2,1,0:T(1,128)S(1)} %convert_element_type.207) | copy-start | bytes 12292
  22.2 36.5 %copy-start.29 = (f32[512]{0:T(512)}, f32[512]{0:T(512)S(1)}, u32[]{:S(2)}) copy-start(f32[512]{0:T(512)S(1)} %broadcast_multiply_fusion.5) | copy-start | bytes 6148
  23.9 34.7 %copy-start.37 = (f32[512]{0:T(512)}, f32[512]{0:T(512)S(1)}, u32[]{:S(2)}) copy-start(f32[512]{0:T(512)S(1)} %add_rsqrt_fusion.1) | copy-start | bytes 6148
  74.7 52.0 %all-to-all-start = ((bf16[512,3,4,256]{3,0,1,2:T(8,128)(2,1)}), bf16[512,3,4,256]{3,0,1,2:T(8,128)(2,1)S(1)}, u32[]{:S(2)}, u32[]{:S(2)}) async-start(bf16[512,3,4,256]{3,0,1,2:T(8,128)(2,1)} %copy.97), calls=%async_computation | async-start | bytes 6291456 | tf_op jit(solution)/shard_map/all_to_all | solution.py:111
  78.5 147.1 %all-gather.11.cloned.1.call-start = ((), (), s32[]{:S(2)}) async-start(), calls=%async_computation.12 | async-start | bytes 2621440 | tf_op jit(solution)/shard_map/all_gather | solution.py:86
  131.9 71.4 %copy-start.45 = (bf16[256]{0:T(256)(128)(2,1)S(1)}, bf16[256]{0:T(256)(128)(2,1)}, u32[]{:S(2)}) copy-start(bf16[256]{0:T(256)(128)(2,1)} %param.24) | copy-start | bytes 1540
  131.9 71.4 %copy-start.46 = (bf16[256]{0:T(256)(128)(2,1)S(1)}, bf16[256]{0:T(256)(128)(2,1)}, u32[]{:S(2)}) copy-start(bf16[256]{0:T(256)(128)(2,1)} %param.25) | copy-start | bytes 1540
  131.9 92.0 %copy-start.20 = (s32[512,1]{0,1:T(1,128)S(1)}, s32[512,1]{0,1:T(1,128)}, u32[]{:S(2)}) copy-start(s32[512,1]{0,1:T(1,128)} %param.19) | copy-start | bytes 6148
  199.0 26.6 %copy-start.4 = (bf16[2048,4,64]{0,2,1:T(8,128)(2,1)}, bf16[2048,4,64]{0,2,1:T(8,128)(2,1)S(1)}, u32[]{:S(2)}) copy-start(bf16[2048,4,64]{0,2,1:T(8,128)(2,1)S(1)} %get-tuple-element.574) | copy-start | bytes 3145732
  199.0 26.6 %copy-start.5 = (bf16[2048,4,64]{0,2,1:T(8,128)(2,1)}, bf16[2048,4,64]{0,2,1:T(8,128)(2,1)S(1)}, u32[]{:S(2)}) copy-start(bf16[2048,4,64]{0,2,1:T(8,128)(2,1)S(1)} %get-tuple-element.575) | copy-start | bytes 3145732
  199.0 26.6 %all-to-all-start.1 = ((bf16[4,512,256]{1,2,0:T(8,128)(2,1)}), bf16[4,512,256]{1,2,0:T(8,128)(2,1)}, u32[]{:S(2)}, u32[]{:S(2)}) async-start(bf16[4,512,256]{1,2,0:T(8,128)(2,1)} %bitcast.224), calls=%async_computation.1 | async-start | bytes 2097152 | tf_op jit(solution)/shard_map/all_to_all | solution.py:157
  203.2 87.8 %all-gather.13.cloned.1.call-start = ((), (), s32[]{:S(2)}) async-start(), calls=%async_computation.13 | async-start | bytes 10485760 | tf_op jit(solution)/shard_map/all_gather | solution.py:30
  232.5 64.0 %copy-start.24 = (bf16[256,64]{0,1:T(8,128)(2,1)S(1)}, bf16[256,64]{0,1:T(8,128)(2,1)}, u32[]{:S(2)}) copy-start(bf16[256,64]{0,1:T(8,128)(2,1)} %param.26) | copy-start | bytes 98308
  291.0 189.1 %all-to-all-start.2 = ((bf16[8,4,8,16,1024]{4,3,1,2,0:T(8,128)(2,1)}), bf16[8,4,8,16,1024]{4,3,1,2,0:T(8,128)(2,1)}, u32[]{:S(2)}, u32[]{:S(2)}) async-start(bf16[8,4,8,16,1024]{4,3,1,2,0:T(8,128)(2,1)} %all-gather.13.cloned.1.call-done), calls=%async_computation.2 | async-start | bytes 16777216 | tf_op jit(solution)/shard_map/all_to_all | solution.py:37
  296.5 70.1 %all-gather.15.cloned.1.call-start = ((), (), s32[]{:S(2)}) async-start(), calls=%async_computation.14 | async-start | bytes 10485760 | tf_op jit(solution)/shard_map/all_gather | solution.py:31
  303.7 823.9 %copy-start.13 = (f32[512,64]{0,1:T(8,128)}, f32[512,64]{0,1:T(8,128)S(1)}, u32[]{:S(2)}) copy-start(f32[512,64]{0,1:T(8,128)S(1)} %get-tuple-element.343) | copy-start | bytes 393220
  303.7 823.9 %copy-start.22 = (f32[512]{0:T(512)}, f32[512]{0:T(512)S(1)}, u32[]{:S(2)}) copy-start(f32[512]{0:T(512)S(1)} %get-tuple-element.342) | copy-start | bytes 6148
  303.8 823.9 %copy-start.25 = (f32[512]{0:T(512)}, f32[512]{0:T(512)S(1)}, u32[]{:S(2)}) copy-start(f32[512]{0:T(512)S(1)} %fusion.107) | copy-start | bytes 6148
  303.8 826.3 %copy-start.27 = (f32[512]{0:T(512)}, f32[512]{0:T(512)S(1)}, u32[]{:S(2)}) copy-start(f32[512]{0:T(512)S(1)} %select_reduce_fusion) | copy-start | bytes 6148
  480.1 187.6 %all-to-all-start.4 = ((bf16[8,4,8,16,1024]{4,3,1,2,0:T(8,128)(2,1)}), bf16[8,4,8,16,1024]{4,3,1,2,0:T(8,128)(2,1)}, u32[]{:S(2)}, u32[]{:S(2)}) async-start(bf16[8,4,8,16,1024]{4,3,1,2,0:T(8,128)(2,1)} %all-gather.15.cloned.1.call-done), calls=%async_computation.4 | async-start | bytes 16777216 | tf_op jit(solution)/shard_map/all_to_all | solution.py:38
  485.1 529.4 %all-reduce.15.cloned.1.call-start = ((), (), s32[]{:S(2)}) async-start(), calls=%async_computation.19 | async-start | bytes 33554432
  1018.4 53.8 %all-to-all-start.3 = ((bf16[8,1,8,16,1024]{4,3,1,2,0:T(8,128)(2,1)}), bf16[8,1,8,16,1024]{4,3,1,2,0:T(8,128)(2,1)}, u32[]{:S(2)}, u32[]{:S(2)}) async-start(bf16[8,1,8,16,1024]{4,3,1,2,0:T(8,128)(2,1)} %copy.105), calls=%async_computation.3 | async-start | bytes 4194304 | tf_op jit(solution)/shard_map/all_to_all | solution.py:207
  1072.3 52.4 %all-to-all-start.5 = ((bf16[8,1,8,16,1024]{4,3,1,2,0:T(8,128)(2,1)}), bf16[8,1,8,16,1024]{4,3,1,2,0:T(8,128)(2,1)}, u32[]{:S(2)}, u32[]{:S(2)}) async-start(bf16[8,1,8,16,1024]{4,3,1,2,0:T(8,128)(2,1)} %copy.108), calls=%async_computation.5 | async-start | bytes 4194304 | tf_op jit(solution)/shard_map/all_to_all | solution.py:210
  1081.3 48.8 %copy-start.42 = (f32[512]{0:T(512)}, f32[512]{0:T(512)S(1)}, u32[]{:S(2)}) copy-start(f32[512]{0:T(512)S(1)} %get-tuple-element.344) | copy-start | bytes 6148
  1134.4 18.0 %all-to-all-start.6 = ((bf16[512,4,256]{2,0,1:T(8,128)(2,1)}), bf16[512,4,256]{2,0,1:T(8,128)(2,1)S(1)}, u32[]{:S(2)}, u32[]{:S(2)}) async-start(bf16[512,4,256]{2,0,1:T(8,128)(2,1)} %bitcast.187), calls=%async_computation.6 | async-start | bytes 2097152 | tf_op jit(solution)/shard_map/all_to_all | solution.py:235
  1137.9 325.2 %reduce-scatter.12.cloned.1.call-start = ((), (), s32[]{:S(2)}) async-start(), calls=%async_computation.16 | async-start | bytes 2621440 | tf_op jit(solution)/shard_map/reduce_scatter | solution.py:293
  1142.5 351.1 %reduce-scatter.10.cloned.1.call-start = ((), (), s32[]{:S(2)}) async-start(), calls=%async_computation.15 | async-start | bytes 7864320 | tf_op jit(solution)/shard_map/reduce_scatter | solution.py:290
  1195.3 7.1 copy-start
  1245.5 7.1 copy-start
  1296.4 7.1 copy-start
  1303.6 4.7 copy-start.19
  1347.4 7.1 copy-start
  1424.3 4.7 copy-start.6
  1424.3 4.7 copy-start.30
  1424.3 4.7 copy-start.33
  1424.3 4.7 copy-start.38
  1424.3 4.7 copy-start.41
  1437.0 92.0 %reduce-scatter.14.cloned.1.call-start = ((), (), s32[]{:S(2)}) async-start(), calls=%async_computation.17 | async-start | bytes 163840 | tf_op jit(solution)/shard_map/reduce_scatter | solution.py:296
  1439.5 183.9 %all-reduce.13.cloned.1.call-start = ((), (), s32[]{:S(2)}) async-start(), calls=%async_computation.18 | async-start | bytes 4194304 | tf_op jit(solution)/shard_map/psum | solution.py:313
  1493.6 20.0 %copy-start.7 = (bf16[512,1024]{1,0:T(8,128)(2,1)S(1)}, bf16[512,1024]{1,0:T(8,128)(2,1)}, u32[]{:S(2)}) copy-start(bf16[512,1024]{1,0:T(8,128)(2,1)} %param.17) | copy-start | bytes 3145732
  1493.6 20.0 %copy-start.31 = (f32[512]{0:T(512)S(1)}, f32[512]{0:T(512)}, u32[]{:S(2)}) copy-start(f32[512]{0:T(512)} %copy-done.29) | copy-start | bytes 6148
  1493.6 20.0 %copy-start.34 = (f32[4,1,256]{2,1,0:T(1,128)S(1)}, f32[4,1,256]{2,1,0:T(1,128)}, u32[]{:S(2)}) copy-start(f32[4,1,256]{2,1,0:T(1,128)} %copy-done.32) | copy-start | bytes 12292
  1493.6 20.0 %copy-start.39 = (f32[512]{0:T(512)S(1)}, f32[512]{0:T(512)}, u32[]{:S(2)}) copy-start(f32[512]{0:T(512)} %copy-done.37) | copy-start | bytes 6148
  1513.7 9.2 copy-start.35
  1513.7 9.2 copy-start.36
  1513.7 57.7 %copy-start.9 = (f32[512,1024]{1,0:T(8,128)S(1)}, f32[512,1024]{1,0:T(8,128)}, u32[]{:S(2)}) copy-start(f32[512,1024]{1,0:T(8,128)} %copy-done.8) | copy-start | bytes 6291460
  (31 other events, 96.0 us)
Sparse Core Ops, SparseCore 0:
  9.6 49.0 all-gather.8
  80.9 35.3 all-gather.10
  232.7 58.2 all-gather.12
  307.9 58.7 all-gather.14
  727.5 286.9 all-reduce.14
  1142.6 30.9 reduce-scatter.11
  1437.1 56.4 reduce-scatter.9
  1496.6 19.5 reduce-scatter.13
  1520.3 103.1 all-reduce.12
where the time goes:
time: 1640 us
  waiting for transfers between devices  934 us (57%)
  matrix products  356 us (22%)
  blocking collectives  135 us (8%)
  other arithmetic  95.7 us (6%)
  local copies, waits for them, and re-layouts  53.1 us (3%)
  starting transfers between devices  33.2 us (2%)
    unnamed x10, waiting for transfers between devices  287 us
    all_to_all x1, waiting for transfers between devices, route_rows(): lax.all_to_all(grads_part, 'dp', split_axis=0, concat_axis=0, tiled=True)  158 us
    all_to_all x1, waiting for transfers between devices, route_rows(): lax.all_to_all(rows_part, 'dp', split_axis=0, concat_axis=0, tiled=True)  113 us
    all_gather x1, waiting for transfers between devices, collect_rows(): lax.all_gather(grads_part, 'seq', axis=1, tiled=True)  58.9 us
    all_gather x1, waiting for transfers between devices, collect_rows(): lax.all_gather(rows_part, 'seq', axis=1, tiled=True)  58.4 us
    all_to_all x1, blocking collectives, per_device(): lax.all_to_all(grad_qkv_heads, 'seq', split_axis=0, concat_axis=2, tiled=...  51.9 us
    psum x1, waiting for transfers between devices, per_device(): lax.psum(summed[0].astype(jnp.bfloat16), 'dp').astype(jnp.float32)  48.4 us
    all_to_all x1, waiting for transfers between devices, per_device(): lax.all_to_all(qkv_local.reshape(row_count, 3, seq_count, head_width), 's...  47.3 us
  transfers between devices with their start and end apart: 16, of which 12 were waited for; matrix products, arithmetic and copies ran while one was open for 25% of the time, Pallas kernels for 0%

commit v1 on v0

v1 whole, which is shorter than its diff:
```python
import functools
import jax
import jax.numpy as jnp
from jax import lax
from jax.experimental import pallas as pl
from jax.experimental.pallas import tpu as pltpu
from jax.sharding import PartitionSpec as P

HD = 64
NEG = -1e30


def _contract(left, right, dims):
    return lax.dot_general(left, right, ((dims[0:1], dims[1:2]), ((), ())), preferred_element_type=jnp.float32)


def _lanes(block, odd):
    lane = lax.broadcasted_iota(jnp.int32, block.shape, 1)
    keep = (lane >= HD) if odd else (lane < HD)
    return jnp.where(keep, block, jnp.zeros_like(block))


def attend_kernel(lows, qkv_ref, first_ref, out_ref, lse_ref, *, rows, keys, width, span):
    index = pl.program_id(0)
    begin = index * rows
    first = first_ref[:, pl.ds(pl.multiple_of(begin, rows), rows)]
    reach = begin + lax.broadcasted_iota(jnp.int32, (1, rows), 1) - first
    low = lows[index]
    high = (begin + rows + keys - 1) // keys
    begin = pl.multiple_of(begin, rows)
    for group in range(width // 128 // span):
        heads = [(group * span + i // 2, i % 2) for i in range(2 * span)]
        queries = [
            _lanes(qkv_ref[pl.ds(begin, rows), pair * 128 : pair * 128 + 128], odd) * (HD ** (-0.5))
            for pair, odd in heads
        ]

        def step(block, carry):
            start = pl.multiple_of(block * keys, keys)
            offset = start + lax.broadcasted_iota(jnp.int32, (keys, rows), 0) - first
            allowed = (offset >= 0) & (offset <= reach)
            fresh = []
            for (pair, odd), q_head, (top, total, acc) in zip(heads, queries, carry):
                column = pair * 128
                k_block = qkv_ref[pl.ds(start, keys), width + column : width + column + 128]
                v_block = qkv_ref[pl.ds(start, keys), 2 * width + column : 2 * width + column + 128]
                scores = jnp.where(allowed, _contract(k_block, q_head, (1, 1)), NEG)
                new_top = jnp.maximum(top, jnp.max(scores, axis=0, keepdims=True))
                weights = jnp.exp(scores - new_top)
                shrink = jnp.exp(top - new_top)
                total = total * shrink + jnp.sum(weights, axis=0, keepdims=True)
                acc = acc * shrink + _contract(v_block, weights.astype(jnp.bfloat16), (0, 0))
                fresh.append((new_top, total, acc))
            return fresh

        done = lax.fori_loop(
            low,
            high,
            step,
            [
                (
                    jnp.full((1, rows), NEG, jnp.float32),
                    jnp.zeros((1, rows), jnp.float32),
                    jnp.zeros((128, rows), jnp.float32),
                )
                for _ in heads
            ],
        )
        halves = []
        for (pair, odd), (top, total, acc) in zip(heads, done):
            lse_ref[2 * pair + odd, :, :] = top + jnp.log(total)
            halves.append((acc * (1.0 / total))[odd * HD : (odd + 1) * HD])
        joined = jnp.concatenate(halves, axis=0)
        out_ref[:, group * span * 128 : (group + 1) * span * 128] = joined.T.astype(jnp.bfloat16)


def attend(qkv, first, lows, rows, keys, span=2):
    length, width = qkv.shape[0], qkv.shape[1] // 3
    heads = width // HD
    return pl.pallas_call(
        functools.partial(attend_kernel, rows=rows, keys=keys, width=width, span=span),
        grid_spec=pltpu.PrefetchScalarGridSpec(
            num_scalar_prefetch=1,
            grid=(length // rows,),
            in_specs=[
                pl.BlockSpec((length, 3 * width), lambda i, lows: (0, 0)),
                pl.BlockSpec((1, length), lambda i, lows: (0, 0)),
            ],
            out_specs=[
                pl.BlockSpec((rows, width), lambda i, lows: (i, 0)),
                pl.BlockSpec((heads, 1, rows), lambda i, lows: (0, 0, i)),
            ],
        ),
        out_shape=[
            jax.ShapeDtypeStruct((length, width), jnp.bfloat16),
            jax.ShapeDtypeStruct((heads, 1, length), jnp.float32),
        ],
        compiler_params=pltpu.CompilerParams(vmem_limit_bytes=48 << 20),
        cost_estimate=pl.CostEstimate(
            flops=2 * heads * length * length * 128, bytes_accessed=8 * length * width, transcendentals=heads * length * length // 2
        ),
        name="attend",
    )(lows, qkv, first)


def attend_back_kernel(
    lows, qkv_ref, first_ref, lse_ref, out_ref, grad_ref, dqkv_ref, dk_acc, dv_acc, *, rows, keys, width, span
):
    index = pl.program_id(0)
    length = qkv_ref.shape[0]

    @pl.when(index == 0)
    def _():
        dk_acc[...] = jnp.zeros_like(dk_acc)
        dv_acc[...] = jnp.zeros_like(dv_acc)

    begin = pl.multiple_of(index * rows, rows)
    first = first_ref[:, pl.ds(begin, rows)]
    reach = begin + lax.broadcasted_iota(jnp.int32, (1, rows), 1) - first
    low = lows[index]
    high = (begin + rows + keys - 1) // keys
    for group in range(width // 128 // span):
        heads = [(group * span + i // 2, i % 2) for i in range(2 * span)]
        fixed = []
        for pair, odd in heads:
            columns = slice(pair * 128, pair * 128 + 128)
            g_pair = grad_ref[pl.ds(begin, rows), columns]
            o_pair = out_ref[pl.ds(begin, rows), columns]
            products = _lanes(g_pair.astype(jnp.float32) * o_pair.astype(jnp.float32), odd).T
            fixed.append(
                (
                    _lanes(qkv_ref[pl.ds(begin, rows), columns], odd) * (HD ** (-0.5)),
                    _lanes(g_pair, odd),
                    lse_ref[2 * pair + odd, :, pl.ds(begin, rows)],
                    jnp.sum(products, axis=0, keepdims=True),
                )
            )

        def step(block, carry):
            start = pl.multiple_of(block * keys, keys)
            offset = start + lax.broadcasted_iota(jnp.int32, (keys, rows), 0) - first
            allowed = (offset >= 0) & (offset <= reach)
            fresh = []
            for (pair, odd), (q_head, g_head, lse, row_dot), dq in zip(heads, fixed, carry):
                column = pair * 128
                k_block = qkv_ref[pl.ds(start, keys), width + column : width + column + 128]
                v_block = qkv_ref[pl.ds(start, keys), 2 * width + column : 2 * width + column + 128]
                scores = jnp.where(allowed, _contract(k_block, q_head, (1, 1)), NEG)
                weights = jnp.exp(scores - lse)
                grad_weights = _contract(v_block, g_head, (1, 1))
                grad_scores = (weights * (grad_weights - row_dot)).astype(jnp.bfloat16)
                dv_acc[pl.ds(start, keys), column : column + 128] += _contract(
                    weights.astype(jnp.bfloat16), g_head, (1, 0)
                )
                dk_acc[pl.ds(start, keys), column : column + 128] += _contract(grad_scores, q_head, (1, 0))
                fresh.append(dq + _contract(k_block, grad_scores, (0, 0)))
            return fresh

        done = lax.fori_loop(low, high, step, [jnp.zeros((128, rows), jnp.float32) for _ in heads])
        joined = jnp.concatenate(
            [dq[odd * HD : (odd + 1) * HD] for (_, odd), dq in zip(heads, done)], axis=0
        ) * (HD ** (-0.5))
        dqkv_ref[pl.ds(begin, rows), group * span * 128 : (group + 1) * span * 128] = joined.T.astype(jnp.bfloat16)

    @pl.when(index == pl.num_programs(0) - 1)
    def _():
        dqkv_ref[:, width : 2 * width] = dk_acc[...].astype(jnp.bfloat16)
        dqkv_ref[:, 2 * width :] = dv_acc[...].astype(jnp.bfloat16)


def attend_back(qkv, first, lse, out, grad, lows, rows, keys, span=2):
    length, width = qkv.shape[0], qkv.shape[1] // 3
    heads = width // HD
    whole = lambda shape: pl.BlockSpec(shape, lambda i, lows: (0,) * len(shape))
    return pl.pallas_call(
        functools.partial(attend_back_kernel, rows=rows, keys=keys, width=width, span=span),
        grid_spec=pltpu.PrefetchScalarGridSpec(
            num_scalar_prefetch=1,
            grid=(length // rows,),
            in_specs=[
                whole((length, 3 * width)),
                whole((1, length)),
                whole((heads, 1, length)),
                whole((length, width)),
                whole((length, width)),
            ],
            out_specs=whole((length, 3 * width)),
            scratch_shapes=[pltpu.VMEM((length, width), jnp.float32)] * 2,
        ),
        out_shape=jax.ShapeDtypeStruct((length, 3 * width), jnp.bfloat16),
        compiler_params=pltpu.CompilerParams(vmem_limit_bytes=56 << 20),
        cost_estimate=pl.CostEstimate(
            flops=5 * heads * length * length * 128, bytes_accessed=18 * length * width, transcendentals=heads * length * length // 2
        ),
        name="attend_back",
    )(lows, qkv, first, lse, out, grad)


EXPERTS = 64
MESH = pl.DeviceIdType.MESH


def moe_kernel(
    send_ref,
    router_ref,
    win_ref,
    wout_ref,
    back_ref,
    rows_out,
    scaled_out,
    hidden_out,
    dpre_out,
    held,
    near,
    far,
    parts,
    relay,
    own,
    final,
    win_buf,
    wout_buf,
    scaled_buf,
    hidden_buf,
    dpre_buf,
    disp_send,
    disp_recv,
    core_send,
    core_recv,
    pair_send,
    pair_recv,
    pass_send,
    pass_recv,
    half_send,
    half_recv,
    rest_send,
    rest_recv,
    back_send,
    back_recv,
    load_sem,
    store_sem,
    rows_sem,
    local_sem,
    *,
    dp_count,
    seq_count,
    local,
    cap,
    group,
    tile,
):
    chunks = local * (dp_count // group)
    parts_of = dp_count // group
    me, my_seq = lax.axis_index("dp"), lax.axis_index("seq")
    my_part = me // group
    lane = me % group
    mate, pair = my_seq + 1 - 2 * (my_seq % 2), (my_seq + 2) % 4
    block = group * cap
    total = seq_count * block
    depth = send_ref.shape[3] // 2
    inner = win_ref.shape[2]

    barrier = pltpu.get_barrier_semaphore()

    def greet(k, _):
        pl.semaphore_signal(barrier, inc=1, device_id=((me + k) % dp_count, my_seq), device_id_type=MESH)
        return 0

    lax.fori_loop(1, dp_count, greet, 0)
    pl.semaphore_signal(barrier, inc=1, device_id=(me, mate), device_id_type=MESH)
    pl.semaphore_signal(barrier, inc=1, device_id=(me, pair), device_id_type=MESH)

    def block_of(seq):
        return pl.ds(pl.multiple_of(seq * block, block), block)

    def load(chunk):
        slot = chunk % 2
        expert = chunk // parts_of
        return (
            pltpu.make_async_copy(win_ref.at[expert], win_buf.at[slot], load_sem.at[slot, 0]),
            pltpu.make_async_copy(wout_ref.at[expert], wout_buf.at[slot], load_sem.at[slot, 1]),
        )

    def dispatch(expert, peer):
        chunk = expert * parts_of + my_part
        place = pl.ds(pl.multiple_of(my_seq * block + lane * cap, cap), cap)
        return pltpu.make_async_remote_copy(
            src_ref=send_ref.at[peer, expert],
            dst_ref=held.at[chunk, place],
            send_sem=disp_send.at[chunk],
            recv_sem=disp_recv.at[chunk],
            device_id=(peer, my_seq),
            device_id_type=MESH,
        )

    def start_dispatch(chunk):
        @pl.when(chunk % parts_of == my_part)
        def _():
            expert = chunk // parts_of
            place = pl.ds(pl.multiple_of(my_seq * block + lane * cap, cap), cap)
            pltpu.make_async_copy(
                send_ref.at[me, expert], held.at[chunk, place], disp_recv.at[chunk]
            ).start()

            def one(k, _):
                dispatch(expert, (me + k) % dp_count).start()
                return 0

            lax.fori_loop(1, dp_count, one, 0)

    def wait_bytes(ref, sem):
        pltpu.make_async_copy(ref, ref, sem).wait()

    def gather_copy(chunk, seq, target, send_sem, recv_sem):
        return pltpu.make_async_remote_copy(
            src_ref=held.at[chunk, block_of(seq)],
            dst_ref=held.at[chunk, block_of(seq)],
            send_sem=send_sem.at[chunk],
            recv_sem=recv_sem.at[chunk],
            device_id=(me, target),
            device_id_type=MESH,
        )

    def start_gather(chunk):
        wait_bytes(held.at[chunk, block_of(my_seq)], disp_recv.at[chunk])
        gather_copy(chunk, my_seq, pair, pair_send, pair_recv).start()
        gather_copy(chunk, my_seq, mate, core_send, core_recv).start()

    def start_pass(chunk):
        gather_copy(chunk, my_seq, pair, pair_send, pair_recv).wait_recv()
        gather_copy(chunk, pair, mate, pass_send, pass_recv).start()

    def half_copy(chunk, side):
        return pltpu.make_async_remote_copy(
            src_ref=parts.at[chunk % 2, block_of(2 * side + mate % 2)],
            dst_ref=near.at[chunk, side],
            send_sem=half_send.at[chunk, side],
            recv_sem=half_recv.at[chunk, side],
            device_id=(me, mate),
            device_id_type=MESH,
        )

    def rest_copy(chunk):
        return pltpu.make_async_remote_copy(
            src_ref=relay.at[chunk % 2],
            dst_ref=far.at[chunk],
            send_sem=rest_send.at[chunk],
            recv_sem=rest_recv.at[chunk],
            device_id=(me, pair),
            device_id_type=MESH,
        )

    def back_copy(chunk, peer):
        expert = chunk // parts_of
        return pltpu.make_async_remote_copy(
            src_ref=final.at[chunk % 2, pl.ds(pl.multiple_of((peer % group) * cap, cap), cap)],
            dst_ref=back_ref.at[me, expert],
            send_sem=back_send.at[chunk],
            recv_sem=back_recv.at[expert],
            device_id=(peer, my_seq),
            device_id_type=MESH,
        )

    def back_local(chunk):
        expert = chunk // parts_of
        return pltpu.make_async_copy(
            final.at[chunk % 2, pl.ds(pl.multiple_of(lane * cap, cap), cap)],
            back_ref.at[me, expert],
            local_sem.at[chunk % 2],
        )

    def rows_copy(chunk):
        return pltpu.make_async_copy(held.at[chunk, :, pl.ds(0, depth)], rows_out.at[chunk], rows_sem.at[chunk])

    def stores(chunk):
        slot = chunk % 2
        return (
            pltpu.make_async_copy(scaled_buf.at[slot], scaled_out.at[chunk], store_sem.at[slot, 0]),
            pltpu.make_async_copy(hidden_buf.at[slot], hidden_out.at[chunk], store_sem.at[slot, 1]),
            pltpu.make_async_copy(dpre_buf.at[slot], dpre_out.at[chunk], store_sem.at[slot, 2]),
        )

    def compute(chunk):
        slot = chunk % 2
        expert = me * local + chunk // parts_of
        gather_copy(chunk, my_seq, mate, core_send, core_recv).wait_recv()
        gather_copy(chunk, pair, mate, pass_send, pass_recv).wait_recv()
        rows_copy(chunk).start()
        rows = held[chunk, :, 0:depth]
        logits = jnp.dot(rows, router_ref[...], preferred_element_type=jnp.float32)
        lanes = lax.broadcasted_iota(jnp.int32, logits.shape, 1)
        logits = jnp.where(lanes < EXPERTS, logits, NEG)
        weights = jnp.exp(logits - jnp.max(logits, axis=1, keepdims=True))
        chosen = jnp.sum(jnp.where(lanes == expert, weights, 0.0), axis=1, keepdims=True)
        gate = chosen / jnp.sum(weights, axis=1, keepdims=True)

        @pl.when(chunk >= 2)
        def _():
            for copy in stores(chunk - 2):
                copy.wait()

        scaled_buf[slot] = (held[chunk, :, depth : 2 * depth].astype(jnp.float32) * gate).astype(jnp.bfloat16)
        for copy in load(chunk):
            copy.wait()

        def first(index, _):
            columns = pl.ds(pl.multiple_of(index * tile, tile), tile)
            pre = jnp.dot(held[chunk, :, 0:depth], win_buf[slot, :, columns], preferred_element_type=jnp.float32)
            back = lax.dot_general(
                scaled_buf[slot],
                wout_buf[slot, columns, :],
                (((1,), (1,)), ((), ())),
                preferred_element_type=jnp.float32,
            )
            root = 0.7978845608028654
            square = pre * pre
            curve = jnp.tanh(root * pre * (1.0 + 0.044715 * square))
            upper = 0.5 * (1.0 + curve)
            slope = upper + (0.5 * root) * pre * (1.0 - curve * curve) * (1.0 + (3 * 0.044715) * square)
            hidden_buf[slot, :, columns] = (pre * upper).astype(jnp.bfloat16)
            dpre_buf[slot, :, columns] = (back * slope).astype(jnp.bfloat16)
            return 0

        lax.fori_loop(0, inner // tile, first, 0)
        for copy in stores(chunk):
            copy.start()

        def second(index, _):
            columns = pl.ds(pl.multiple_of(index * tile, tile), tile)
            parts[slot, :, columns] = jnp.dot(
                hidden_buf[slot], wout_buf[slot, :, columns], preferred_element_type=jnp.float32
            ).astype(jnp.bfloat16)
            others = pl.ds(pl.multiple_of(depth + index * tile, tile), tile)
            parts[slot, :, others] = lax.dot_general(
                dpre_buf[slot],
                win_buf[slot, columns, :],
                (((1,), (1,)), ((), ())),
                preferred_element_type=jnp.float32,
            ).astype(jnp.bfloat16)
            return 0

        lax.fori_loop(0, depth // tile, second, 0)
        for side in range(2):
            half_copy(chunk, side).start()

    def start_rest(chunk):
        slot = chunk % 2
        for side in range(2):
            half_copy(chunk, side).wait()
        far_side, my_side = pair // 2, my_seq // 2

        @pl.when(chunk >= 2)
        def _():
            rest_copy(chunk - 2).wait_send()

        relay[slot] = (
            parts[slot, block_of(pair)].astype(jnp.float32) + near[chunk, far_side].astype(jnp.float32)
        ).astype(jnp.bfloat16)
        rest_copy(chunk).start()
        own[slot] = parts[slot, block_of(my_seq)].astype(jnp.float32) + near[chunk, my_side].astype(jnp.float32)

    def wait_back(chunk):
        @pl.when(chunk % parts_of == my_part)
        def _():
            wait_bytes(final.at[0, pl.ds(0, (group - 1) * cap)], back_send.at[chunk])
            back_local(chunk).wait()

        @pl.when(chunk % parts_of != my_part)
        def _():
            wait_bytes(final.at[0], back_send.at[chunk])

    def start_back(chunk):
        slot = chunk % 2
        part = chunk % parts_of
        rest_copy(chunk).wait_recv()

        @pl.when(chunk >= 2)
        def _():
            wait_back(chunk - 2)

        final[slot] = (own[slot] + far[chunk].astype(jnp.float32)).astype(jnp.bfloat16)

        def one(k, _):
            peer = part * group + (lane + k) % group

            @pl.when(peer == me)
            def _():
                back_local(chunk).start()

            @pl.when(peer != me)
            def _():
                back_copy(chunk, peer).start()

            return 0

        lax.fori_loop(0, group, one, 0)

    for copy in load(0):
        copy.start()
    pl.semaphore_wait(barrier, dp_count + 1)

    def step(time, _):
        @pl.when(time < chunks)
        def _():
            start_dispatch(time)

        @pl.when((time >= 1) & (time < chunks + 1))
        def _():
            start_gather(time - 1)

        @pl.when((time >= 2) & (time < chunks + 2))
        def _():
            start_pass(time - 2)

        @pl.when((time >= 4) & (time < chunks + 4))
        def _():
            start_rest(time - 4)

        @pl.when((time >= 5) & (time < chunks + 5))
        def _():
            start_back(time - 5)

        @pl.when((time >= 3) & (time < chunks + 3))
        def _():
            chunk = time - 3

            @pl.when(chunk + 1 < chunks)
            def _():
                for copy in load(chunk + 1):
                    copy.start()

            compute(chunk)

        return 0

    lax.fori_loop(0, chunks + 5, step, 0)

    def drain(chunk, _):
        @pl.when(chunk % parts_of == my_part)
        def _():
            wait_bytes(send_ref.at[pl.ds(0, dp_count - 1), 0], disp_send.at[chunk])

        gather_copy(chunk, my_seq, pair, pair_send, pair_recv).wait_send()
        gather_copy(chunk, my_seq, mate, core_send, core_recv).wait_send()
        gather_copy(chunk, pair, mate, pass_send, pass_recv).wait_send()
        rows_copy(chunk).wait()

        @pl.when(chunk >= chunks - 2)
        def _():
            for copy in stores(chunk):
                copy.wait()
            rest_copy(chunk).wait_send()
            wait_back(chunk)

        return 0

    lax.fori_loop(0, chunks, drain, 0)

    def arrive(expert, _):
        wait_bytes(back_ref.at[pl.ds(0, dp_count - 1), expert], back_recv.at[expert])
        return 0

    lax.fori_loop(0, local, arrive, 0)


def experts_exchange(send, router, w_in, w_out):
    dp_count, local, cap, width = send.shape
    width = width // 2
    inner = w_in.shape[2]
    seq_count = lax.axis_size("seq")
    group = min(8, dp_count)
    chunks = local * (dp_count // group)
    block = group * cap
    total = seq_count * block
    tile = 256
    bf = jnp.bfloat16
    anywhere = pl.BlockSpec(memory_space=pl.ANY)
    dma = pltpu.SemaphoreType.DMA
    flops = 2 * 4 * chunks * total * width * inner
    return pl.pallas_call(
        functools.partial(
            moe_kernel, dp_count=dp_count, seq_count=seq_count, local=local, cap=cap, group=group, tile=tile
        ),
        in_specs=[anywhere, pl.BlockSpec(memory_space=pltpu.VMEM), anywhere, anywhere],
        out_specs=[anywhere] * 5,
        out_shape=[
            jax.ShapeDtypeStruct(send.shape, bf),
            jax.ShapeDtypeStruct((chunks, total, width), bf),
            jax.ShapeDtypeStruct((chunks, total, width), bf),
            jax.ShapeDtypeStruct((chunks, total, inner), bf),
            jax.ShapeDtypeStruct((chunks, total, inner), bf),
        ],
        scratch_shapes=[
            pltpu.VMEM((chunks, total, 2 * width), bf),
            pltpu.VMEM((chunks, 2, block, 2 * width), bf),
            pltpu.VMEM((chunks, block, 2 * width), bf),
            pltpu.VMEM((2, total, 2 * width), bf),
            pltpu.VMEM((2, block, 2 * width), bf),
            pltpu.VMEM((2, block, 2 * width), jnp.float32),
            pltpu.VMEM((2, block, 2 * width), bf),
            pltpu.VMEM((2, width, inner), bf),
            pltpu.VMEM((2, inner, width), bf),
            pltpu.VMEM((2, total, width), bf),
            pltpu.VMEM((2, total, inner), bf),
            pltpu.VMEM((2, total, inner), bf),
            dma((chunks,)),
            dma((chunks,)),
            dma((chunks,)),
            dma((chunks,)),
            dma((chunks,)),
            dma((chunks,)),
            dma((chunks,)),
            dma((chunks,)),
            dma((chunks, 2)),
            dma((chunks, 2)),
            dma((chunks,)),
            dma((chunks,)),
            dma((chunks,)),
            dma((local,)),
            dma((2, 2)),
            dma((2, 3)),
            dma((chunks,)),
            dma((2,)),
        ],
        compiler_params=pltpu.CompilerParams(
            collective_id=1, has_side_effects=True, vmem_limit_bytes=62 << 20
        ),
        cost_estimate=pl.CostEstimate(flops=flops, bytes_accessed=96 << 20, transcendentals=0),
        name="experts",
    )(send, router, w_in, w_out)


H = 16
EPS = 1e-05
PACK_ROWS = 80


def normalize(values):
    center = values - jnp.mean(values, axis=-1, keepdims=True)
    inverse = lax.rsqrt(jnp.mean(center * center, axis=-1, keepdims=True) + EPS)
    return (center * inverse, inverse)


def norm_back(grad_norm, normed, inverse):
    first_mean = jnp.mean(grad_norm, axis=-1, keepdims=True)
    second_mean = jnp.mean(grad_norm * normed, axis=-1, keepdims=True)
    return inverse * (grad_norm - first_mean - normed * second_mean)


def dot(left, right, dims):
    return lax.dot_general(left, right, ((dims[0:1], dims[1:2]), ((), ())), preferred_element_type=jnp.float32)


def per_device(
    tokens,
    doc_starts,
    routes,
    ln1_gain,
    ln1_bias,
    w_qkv,
    w_proj,
    ln2_gain,
    ln2_bias,
    w_router,
    w_expert_in,
    w_expert_out,
    out_grad,
):
    seq_count = lax.axis_size("seq")
    dp_count = lax.axis_size("dp")
    seq_index = lax.axis_index("seq")
    row_count, width = tokens.shape
    length = row_count * seq_count
    shard = width // seq_count
    head_width = H // seq_count * HD
    local_experts = EXPERTS // dp_count
    capacity = max(2, 2 * row_count // EXPERTS)

    expert_ids = routes[:, 0]
    selector = expert_ids[:, None] == jnp.arange(EXPERTS, dtype=jnp.int32)[None, :]
    selector_float = selector.astype(jnp.float32)
    row_range = jnp.arange(row_count, dtype=jnp.int32)
    earlier = (row_range[:, None] > row_range[None, :]).astype(jnp.bfloat16)
    counts = jnp.dot(earlier, selector.astype(jnp.bfloat16), preferred_element_type=jnp.float32)
    ranking = jnp.sum(counts * selector_float, axis=1).astype(jnp.int32)
    slot_ids = expert_ids * capacity + ranking
    placement = (
        jnp.arange(EXPERTS * capacity, dtype=jnp.int32)[:, None] == slot_ids[None, :]
    ).astype(jnp.bfloat16)

    small = jnp.concatenate(
        [
            w_router.T,
            jnp.stack([ln1_gain, ln1_bias, ln2_gain, ln2_bias]),
            jnp.zeros((PACK_ROWS - EXPERTS - 4, shard), jnp.bfloat16),
        ],
        axis=0,
    )
    small_all = lax.all_gather(small, "seq", axis=1, tiled=True)
    router_weight = small_all[:EXPERTS].T
    gains = small_all[EXPERTS : EXPERTS + 4].astype(jnp.float32)
    gain_one, bias_one, gain_two, bias_two = gains[0], gains[1], gains[2], gains[3]
    tokens_all = lax.all_gather(tokens, "seq", axis=0, tiled=True)
    qkv_pieces = w_qkv.reshape(shard, 3, seq_count, head_width).transpose(2, 0, 1, 3)
    qkv_weight = lax.all_to_all(
        qkv_pieces.reshape(seq_count, shard, 3 * head_width), "seq", split_axis=0, concat_axis=0, tiled=True
    ).reshape(width, 3 * head_width)
    proj_weight = lax.all_gather(w_proj, "seq", axis=0, tiled=True)
    normed_all, _ = normalize(tokens_all.astype(jnp.float32))
    hidden_all = (normed_all * gain_one + bias_one).astype(jnp.bfloat16)
    qkv = dot(hidden_all, qkv_weight, (1, 0)).astype(jnp.bfloat16)

    starts = doc_starts[0]
    positions = jnp.arange(length, dtype=jnp.int32)
    doc_first = jnp.max(jnp.where(starts[None, :] <= positions[:, None], starts[None, :], 0), axis=1)
    block = min(512, length)
    lows = doc_first[::block] // block
    heads_out, lse = attend(qkv, doc_first[None, :], lows, block, block)
    token_heads = lax.all_to_all(
        heads_out.reshape(seq_count, row_count, head_width), "seq", split_axis=0, concat_axis=0, tiled=True
    )
    token_heads = token_heads.transpose(1, 0, 2).reshape(row_count, width)

    inputs = tokens.astype(jnp.float32)
    middle = inputs + dot(token_heads, proj_weight, (1, 0))
    normed_two, inverse_two = normalize(middle)
    hidden_two = (normed_two * gain_two + bias_two).astype(jnp.bfloat16)
    both = jnp.concatenate([hidden_two, out_grad], axis=1)
    send = dot(placement, both, (1, 0)).astype(jnp.bfloat16)
    send = send.reshape(dp_count, local_experts, capacity, 2 * width)
    router_wide = jnp.pad(router_weight, ((0, 0), (0, 128 - EXPERTS)))
    back, rows_in, scaled, hidden, grad_pre = experts_exchange(send, router_wide, w_expert_in, w_expert_out)
    logits = dot(hidden_two, router_weight, (1, 0))
    probs = jax.nn.softmax(logits, axis=-1)
    gate = jnp.sum(probs * selector_float, axis=1)
    grad_out = out_grad.astype(jnp.float32)

    by_expert = lambda values: values.reshape(local_experts, -1, values.shape[2])
    expert_in_grad = jnp.einsum(
        "erd,erf->edf", by_expert(rows_in), by_expert(grad_pre), preferred_element_type=jnp.float32
    )
    expert_out_grad = jnp.einsum(
        "erf,erd->efd", by_expert(hidden), by_expert(scaled), preferred_element_type=jnp.float32
    )
    combined = dot(placement, back.reshape(EXPERTS * capacity, 2 * width), (0, 0))
    expert_out, expert_dx = combined[:, :width], combined[:, width:]
    output = (middle + gate[:, None] * expert_out).astype(jnp.bfloat16)
    grad_gate = jnp.sum(grad_out * expert_out, axis=1)
    grad_logits = probs * (selector_float - gate[:, None]) * grad_gate[:, None]
    router_grad = lax.dot_general(
        grad_logits,
        hidden_two.astype(jnp.float32),
        (((0,), (0,)), ((), ())),
        precision=lax.Precision.HIGHEST,
    )
    grad_two = expert_dx + jnp.dot(
        grad_logits, router_weight.astype(jnp.float32).T, precision=lax.Precision.HIGHEST
    )
    gain_two_grad = jnp.sum(grad_two * normed_two, axis=0)
    bias_two_grad = jnp.sum(grad_two, axis=0)
    grad_middle = grad_out + norm_back(grad_two * gain_two, normed_two, inverse_two)
    grad_branch = grad_middle.astype(jnp.bfloat16)
    grad_heads = dot(grad_branch, proj_weight, (1, 1)).astype(jnp.bfloat16)
    grad_heads = lax.all_to_all(
        grad_heads.reshape(row_count, seq_count, head_width).transpose(1, 0, 2),
        "seq",
        split_axis=0,
        concat_axis=0,
        tiled=True,
    ).reshape(length, head_width)
    proj_grad = dot(token_heads, grad_branch, (0, 0))

    early = jnp.concatenate(
        [
            proj_grad.reshape(seq_count, shard, width),
            jnp.concatenate([router_grad, gain_two_grad[None], bias_two_grad[None]], axis=0)
            .reshape(EXPERTS + 2, seq_count, shard)
            .transpose(1, 2, 0),
        ],
        axis=2,
    ).astype(jnp.bfloat16)
    early = lax.psum_scatter(early.reshape(width, width + EXPERTS + 2), "seq", scatter_dimension=0, tiled=True)
    early = lax.psum(early, "dp").astype(jnp.float32)

    grad_qkv = attend_back(qkv, doc_first[None, :], lse, heads_out, grad_heads, lows, block, block)
    grad_one_part = dot(grad_qkv, qkv_weight, (1, 1))
    gain_one_part = jnp.sum(grad_one_part * normed_all, axis=0)
    bias_one_part = jnp.sum(grad_one_part, axis=0)
    grad_one = lax.psum_scatter(
        grad_one_part.astype(jnp.bfloat16), "seq", scatter_dimension=0, tiled=True
    ).astype(jnp.float32)
    qkv_grad = dot(hidden_all, grad_qkv, (0, 0)).astype(jnp.bfloat16)
    ones = jnp.stack([gain_one_part, bias_one_part], axis=1).astype(jnp.bfloat16)
    late = jnp.concatenate([qkv_grad, ones], axis=1).reshape(seq_count, shard, 3 * head_width + 2)
    late = lax.all_to_all(late, "seq", split_axis=0, concat_axis=0, tiled=True)
    ones_sum = jnp.sum(late[:, :, 3 * head_width :].astype(jnp.float32), axis=0).astype(jnp.bfloat16)
    late = late[:, :, : 3 * head_width].reshape(seq_count, shard, 3, head_width).transpose(1, 2, 0, 3)
    late = jnp.concatenate([late.reshape(shard, 3 * width), ones_sum], axis=1)
    late = lax.psum(late, "dp").astype(jnp.float32)

    normed_one, inverse_one = normalize(inputs)
    input_grad = grad_middle + norm_back(grad_one * gain_one, normed_one, inverse_one)
    return (
        output,
        input_grad,
        late[:, 3 * width],
        late[:, 3 * width + 1],
        late[:, : 3 * width],
        early[:, :width],
        early[:, width + EXPERTS],
        early[:, width + EXPERTS + 1],
        early[:, width : width + EXPERTS],
        expert_in_grad,
        expert_out_grad,
    )


def solution(mesh):
    in_specs = (
        P(("dp", "seq"), None),
        P("dp", None),
        P(("dp", "seq"), None),
        P("seq"),
        P("seq"),
        P("seq", None),
        P("seq", None),
        P("seq"),
        P("seq"),
        P("seq", None),
        P("dp", None, "seq"),
        P("dp", "seq", None),
        P(("dp", "seq"), None),
    )
    out_specs = (
        P(("dp", "seq"), None),
        P(("dp", "seq"), None),
        P("seq"),
        P("seq"),
        P("seq", None),
        P("seq", None),
        P("seq"),
        P("seq"),
        P("seq", None),
        P("dp", None, "seq"),
        P("dp", "seq", None),
    )
    return jax.shard_map(
        per_device, mesh=mesh, in_specs=in_specs, out_specs=out_specs, check_vma=False
    )
```

time: 1640 us -> 647 us (0.39)
  waiting for transfers between devices: 934 us -> 124 us
  Pallas kernels: 0 us -> 285 us
  matrix products: 356 us -> 78.7 us
  blocking collectives: 135 us -> 57.9 us
  other arithmetic: 95.7 us -> 24 us
  starting transfers between devices: 33.2 us -> 13 us
    all_to_all x7 -> x3, waiting for transfers between devices: 416 us -> 24.6 us  [the longest x1 13.3 us: per_device(): lax.all_to_all(heads_out.reshape(seq_count, row_count, head_width), 'seq'...]
    unnamed x10 -> x5, waiting for transfers between devices: 287 us -> 1.96 us
    pallas_call x0 -> x3, Pallas kernels: none -> 285 us  [the longest x1 219 us: experts_exchange(): pl.pallas_call(functools.partial(moe_kernel, dp_count=dp_count, seq_count...]
    dot_general x46 -> x13, matrix products: 353 us -> 75 us  [the longest x9 31.5 us: dot(): lax.dot_general(left, right, ((dims[0:1], dims[1:2]), ((), ())), preferre...]
    all_gather x4 -> x2, waiting for transfers between devices: 152 us -> 5.78 us  [the longest x1 5.76 us: per_device(): tokens_all = lax.all_gather(tokens, 'seq', axis=0, tiled=True)]
    convert_element_type x18 -> x2, other arithmetic: 53.9 us -> 2.12 us  [the longest x1 1.99 us: per_device(): late = lax.psum(late, 'dp').astype(jnp.float32)]
    psum x1 -> x0, blocking collectives: 39.5 us -> none  [per_device(): lax.psum(summed[3].astype(jnp.bfloat16), 'dp').astype(jnp.float32)]
    all_to_all x1, blocking collectives: 51.9 us -> 22.7 us  [per_device(): late = lax.all_to_all(late, 'seq', split_axis=0, concat_axis=0, tiled=True)]
  transfers between devices with their start and end apart: 16 -> 8, of which waited for: 12 -> 5; matrix products, arithmetic and copies ran while one was open for 25% -> 17% of each run, Pallas kernels for 0% -> 10%
where the time goes in v1:
time: 647 us; the launch traced here: 639 us
  Pallas kernels  285 us (44%)
  waiting for transfers between devices  124 us (19%)
  matrix products  78.7 us (12%)
  blocking collectives  57.9 us (9%)
  local copies, waits for them, and re-layouts  41.9 us (6%)
  other arithmetic  24 us (4%)
  between operations  14.9 us (2%)
  starting transfers between devices  13 us (2%)
    pallas_call x1, Pallas kernels, experts_exchange(): pl.pallas_call(functools.partial(moe_kernel, dp_count=dp_count, seq_count...  219 us
    psum x1, waiting for transfers between devices, per_device(): early = lax.psum(early, 'dp').astype(jnp.float32)  58.7 us
    pallas_call x1, Pallas kernels, attend_back(): pl.pallas_call(functools.partial(attend_back_kernel, rows=rows, keys=keys...  39.1 us
    all_gather x1, blocking collectives, per_device(): small_all = lax.all_gather(small, 'seq', axis=1, tiled=True)  35.3 us
    reduce_scatter x1, waiting for transfers between devices, per_device(): lax.psum_scatter(grad_one_part.astype(jnp.bfloat16), 'seq', scatter_dimen...  32.7 us
    dot_general x9, matrix products, dot(): lax.dot_general(left, right, ((dims[0:1], dims[1:2]), ((), ())), preferre...  31.5 us
    pallas_call x1, Pallas kernels, attend(): pl.pallas_call(functools.partial(attend_kernel, rows=rows, keys=keys, wid...  26.8 us
    all_to_all x1, blocking collectives, per_device(): late = lax.all_to_all(late, 'seq', split_axis=0, concat_axis=0, tiled=True)  22.7 us
  transfers between devices with their start and end apart: 8, of which 5 were waited for; matrix products, arithmetic and copies ran while one was open for 17% of the time, Pallas kernels for 10%

profile of v1, /device:TPU:0, one launch (start us, length us, event | category | flops | bytes accessed | tf_op | source)
XLA Modules:
  0.0 638.8 jit_solution(7238195939991681800)
XLA Ops:
  7.9 1.7 copy.77
  9.6 1.3 copy.78
  10.9 4.4 all-to-all-start
  17.0 35.3 %all_gather.10 = bf16[80,1024]{0,1:T(8,128)(2,1)S(1)} all-gather(bf16[80,256]{0,1:T(8,128)(2,1)S(1)} %concatenate.31), channel_id=1, replica_groups=mesh['dp'=8,'seq'=4] {'seq'}, dimensions={1}, use_global_device_ids=true | all-gather | bytes 204800 | tf_op jit(solution)/shard_map/all_gather | solution.py:698
  53.5 1.6 copy.79
  55.1 5.8 all-gather.3.cloned.1.call-done
  60.8 3.0 convert_reduce_fusion
  64.3 1.4 fusion.7
  65.7 4.3 convolution_convert_fusion.1.qkv_ref
  70.0 26.8 %attend.1 = (bf16[2048,256]{1,0:T(8,128)(2,1)S(1)}, f32[4,1,2048]{2,1,0:T(1,128)S(1)}) custom-call(s32[4]{0:T(128)S(1)} %and_select_fusion.lows, bf16[2048,768]{1,0:T(8,128)(2,1)S(1)} %convolution_convert_fusion.1.qkv_ref, s32[1,2048]{1,0:T(1,128)S(1)} %bitcast.55), custom_call_target="tpu_custom_call" | custom-call | flops 4294967296 | bytes 4194304 | tf_op jit(solution)/shard_map/attend/pallas_call | solution.py:80
  97.5 1.3 copy.80
  98.8 4.1 all-to-all-start.1
  104.0 13.3 %all-to-all-done.1 = bf16[4,512,256]{1,2,0:T(8,128)(2,1)S(1)} async-done(((bf16[4,512,256]{1,2,0:T(8,128)(2,1)}), bf16[4,512,256]{1,2,0:T(8,128)(2,1)S(1)}, u32[]{:S(2)}, u32[]{:S(2)}) %all-to-all-start.1) | async-done | bytes 1048608 | tf_op jit(solution)/shard_map/all_to_all | solution.py:718
  117.3 3.3 fusion.46
  124.1 4.4 convolution_convert_fusion
  128.4 218.6 %experts.1 = (bf16[8,8,16,2048]{3,2,1,0:T(8,128)(2,1)}, bf16[8,512,1024]{2,1,0:T(8,128)(2,1)}, bf16[8,512,1024]{2,1,0:T(8,128)(2,1)}, bf16[8,512,1024]{2,1,0:T(8,128)(2,1)}, bf16[8,512,1024]{2,1,0:T(8,128)(2,1)}) custom-call(bf16[8,8,16,2048]{3,2,1,0:T(8,128)(2,1)} %bitcast.76, bf16[1024,128]{1,0:T(8,128)(2,1)} %pad.4.router_ref, ...), custom_call_target="tpu_custom_call" | custom-call | flops 34359738368 | bytes 100663296 | tf_op jit(solution)/shard_map/experts/pallas_call | solution.py:579
  347.1 4.9 fusion.22
  352.1 1.4 fusion.17
  353.5 3.7 multiply_reduce_fusion
  360.0 2.7 convert_add_fusion.1
  362.7 1.3 convolution_convert_fusion.4
  365.1 4.4 all-to-all-start.2
  369.7 1.3 convolution_convert_fusion.2
  371.0 1.6 pad_maximum_fusion
  372.7 11.3 %all-to-all-done.2 = bf16[4,512,256]{2,1,0:T(8,128)(2,1)} async-done(((bf16[4,512,256]{2,1,0:T(8,128)(2,1)}), bf16[4,512,256]{2,1,0:T(8,128)(2,1)}, u32[]{:S(2)}, u32[]{:S(2)}) %all-to-all-start.2) | async-done | bytes 1048608 | tf_op jit(solution)/shard_map/all_to_all | solution.py:763
  384.0 39.1 %attend_back.1 = bf16[2048,768]{1,0:T(8,128)(2,1)} custom-call(s32[4]{0:T(128)} %copy-done.2, bf16[2048,768]{1,0:T(8,128)(2,1)} %copy-done.3, s32[1,2048]{1,0:T(1,128)} %bitcast.56, f32[4,1,2048]{2,1,0:T(1,128)} %copy-done.4, bf16[2048,256]{1,0:T(8,128)(2,1)} %copy-done, bf16[2048,256]{1,0:T(8,128)(2,1)} %bitcast.15.grad_ref), custom_call_target="tpu_custom_call" | custom-call | flops 10737418240 | bytes 9437184 | tf_op jit(solution)/shard_map/attend_back/pallas_call | solution.py:175
  423.2 7.4 %fusion.6 = (bf16[1024]{0:T(1024)(128)(2,1)S(1)}, bf16[1024]{0:T(1024)(128)(2,1)S(1)}, bf16[2048,1024]{1,0:T(8,128)(2,1)}) fusion(bf16[2048,1024]{1,0:T(8,128)(2,1)S(1)} %copy-done.10, f32[2048]{0:T(1024)S(1)} %copy-done.34, f32[2048]{0:T(1024)S(1)} %copy-done.23, bf16[2048,768]{1,0:T(8,128)(2,1)} %attend_back.1, bf16[1024,768]{1,0:T(8,128)(2,1)} %bitcast.61), kind=kOutput, calls=%fused_computation.8 | convolution fusion | flops 3235903488 | bytes 13127680 | tf_op jit(solution)/shard_map/dot_general | solution.py:650
  430.6 4.2 convolution_convert_fusion.3
  434.8 1.3 pad_maximum_fusion.2
  436.1 4.2 reshape.149
  440.3 1.6 copy.82
  441.9 22.7 %all_to_all.20 = bf16[4,256,770]{1,2,0:T(8,128)(2,1)S(1)} all-to-all(bf16[4,256,770]{1,2,0:T(8,128)(2,1)S(1)} %copy.82), channel_id=1, replica_groups=mesh['dp'=8,'seq'=4] {'seq'}, dimensions={0} | all-to-all | bytes 3153920 | tf_op jit(solution)/shard_map/all_to_all | solution.py:794
  467.0 3.7 copy.83
  470.8 4.1 reshape.151
  475.7 2.7 pad_maximum_fusion.1
  480.3 21.6 %fusion.48 = f32[8,1024,1024]{2,1,0:T(8,128)} fusion(bf16[8,512,1024]{2,1,0:T(8,128)(2,1)} %get-tuple-element.21, bf16[8,512,1024]{2,1,0:T(8,128)(2,1)} %get-tuple-element.22), kind=kOutput, calls=%fused_computation.104 | convolution fusion | flops 8589934592 | bytes 50331648 | tf_op jit(solution)/shard_map/erd,erf->edf/dot_general | solution.py:738
  501.9 20.9 %fusion.49 = f32[8,1024,1024]{2,1,0:T(8,128)} fusion(bf16[8,512,1024]{2,1,0:T(8,128)(2,1)} %get-tuple-element.23, bf16[8,512,1024]{2,1,0:T(8,128)(2,1)} %get-tuple-element.24), kind=kOutput, calls=%fused_computation.105 | convolution fusion | flops 8589934592 | bytes 50331648 | tf_op jit(solution)/shard_map/erf,erd->efd/dot_general | solution.py:741
  522.9 58.7 %all-reduce.4.cloned.1.call-done = (bf16[256,1090]{0,1:T(8,128)(2,1)}, bf16[256,3074]{1,0:T(8,128)(2,1)}) async-done(((bf16[256,1090]{0,1:T(8,128)(2,1)}, bf16[256,3074]{1,0:T(8,128)(2,1)}), (bf16[256,1090]{0,1:T(8,128)(2,1)}, bf16[256,3074]{1,0:T(8,128)(2,1)})) %all-reduce.4.cloned.1.call-update) | async-done | bytes 2131984 | tf_op jit(solution)/shard_map/psum | solution.py:782
  581.6 1.5 slice.88
  583.1 2.1 slice.85
  585.2 2.0 slice.84
  587.3 2.0 convert_element_type.86
  589.2 2.5 copy.88
  591.8 1.9 slice_reduce_fusion.4
  593.6 1.3 fusion.45
  595.0 32.7 %reduce-scatter.3.cloned.1.call-done = bf16[512,1024]{1,0:T(8,128)(2,1)} async-done(((bf16[2048,1024]{1,0:T(8,128)(2,1)}), bf16[512,1024]{1,0:T(8,128)(2,1)}) %reduce-scatter.3.cloned.1.call-update) | async-done | bytes 1048592 | tf_op jit(solution)/shard_map/reduce_scatter | solution.py:788
  627.7 2.1 fusion.21
  629.8 2.1 fusion.15
  (146 shorter events, 18.5 us)
Async XLA Ops:
  7.2 53.7 %all-gather.3.cloned.1.call-start = ((), (), s32[]{:S(2)}) async-start(), calls=%async_computation.6 | async-start | bytes 5242880 | tf_op jit(solution)/shard_map/all_gather | solution.py:702
  10.9 5.1 copy-start.42
  10.9 5.3 copy-start.38
  10.9 5.4 copy-start.39
  10.9 5.6 copy-start.40
  10.9 5.7 copy-start.41
  10.9 5.8 copy-start.24
  10.9 42.6 %all-to-all-start = ((bf16[4,256,768]{1,2,0:T(8,128)(2,1)}), bf16[4,256,768]{1,2,0:T(8,128)(2,1)S(1)}, u32[]{:S(2)}, u32[]{:S(2)}) async-start(bf16[4,256,768]{1,2,0:T(8,128)(2,1)} %bitcast.4), calls=%async_computation | async-start | bytes 3145728 | tf_op jit(solution)/shard_map/all_to_all | solution.py:704
  15.3 88.8 %all-gather.5.cloned.1.call-start = ((), (), s32[]{:S(2)}) async-start(), calls=%async_computation.7 | async-start | bytes 2621440 | tf_op jit(solution)/shard_map/all_gather | solution.py:707
  16.1 53.9 %copy-start.1 = (s32[2048]{0:T(1024)}, s32[2048]{0:T(1024)S(1)}, u32[]{:S(2)}) copy-start(s32[2048]{0:T(1024)S(1)} %select_reduce_fusion.1) | copy-start | bytes 24580
  53.5 12.2 %copy-start.35 = (f32[1024]{0:T(1024)}, f32[1024]{0:T(1024)S(1)}, u32[]{:S(2)}) copy-start(f32[1024]{0:T(1024)S(1)} %get-tuple-element.92) | copy-start | bytes 12292
  53.5 16.5 %copy-start.2 = (s32[4]{0:T(128)}, s32[4]{0:T(128)S(1)}, u32[]{:S(2)}) copy-start(s32[4]{0:T(128)S(1)} %and_select_fusion.lows) | copy-start | bytes 52
  60.8 3.4 copy-start.9
  64.3 1.4 copy-start.22
  64.3 1.4 copy-start.21
  65.7 4.3 copy-start.33
  70.0 26.8 %copy-start.3 = (bf16[2048,768]{1,0:T(8,128)(2,1)}, bf16[2048,768]{1,0:T(8,128)(2,1)S(1)}, u32[]{:S(2)}) copy-start(bf16[2048,768]{1,0:T(8,128)(2,1)S(1)} %convolution_convert_fusion.1.qkv_ref) | copy-start | bytes 9437188
  97.5 1.3 copy-start
  98.8 4.9 copy-start.30
  98.8 18.5 %copy-start.7 = (bf16[512,1024]{1,0:T(8,128)(2,1)S(1)}, bf16[512,1024]{1,0:T(8,128)(2,1)}, u32[]{:S(2)}) copy-start(bf16[512,1024]{1,0:T(8,128)(2,1)} %param.13) | copy-start | bytes 3145732
  98.8 18.5 %all-to-all-start.1 = ((bf16[4,512,256]{1,2,0:T(8,128)(2,1)}), bf16[4,512,256]{1,2,0:T(8,128)(2,1)S(1)}, u32[]{:S(2)}, u32[]{:S(2)}) async-start(bf16[4,512,256]{1,2,0:T(8,128)(2,1)} %copy.80), calls=%async_computation.1 | async-start | bytes 2097152 | tf_op jit(solution)/shard_map/all_to_all | solution.py:718
  104.0 20.1 %copy-start.37 = (s32[512]{0:T(512)}, s32[512]{0:T(512)S(1)}, u32[]{:S(2)}) copy-start(s32[512]{0:T(512)S(1)} %convert_add_fusion.2) | copy-start | bytes 6148
  117.3 3.3 copy-start.15
  120.7 1.7 copy-start.5
  121.9 1.5 copy-start.31
  121.9 2.1 copy-start.18
  347.1 4.9 copy-start.6
  347.1 4.9 copy-start.19
  347.1 4.9 copy-start.29
  352.0 1.5 copy-start.26
  352.0 1.5 copy-start.28
  352.0 1.5 copy-start.32
  360.0 2.7 copy-start.20
  362.7 1.3 copy-start.12
  364.0 5.7 copy-start.13
  364.0 5.7 copy-start.16
  365.1 18.9 %all-to-all-start.2 = ((bf16[4,512,256]{2,1,0:T(8,128)(2,1)}), bf16[4,512,256]{2,1,0:T(8,128)(2,1)}, u32[]{:S(2)}, u32[]{:S(2)}) async-start(bf16[4,512,256]{2,1,0:T(8,128)(2,1)} %bitcast.53), calls=%async_computation.2 | async-start | bytes 2097152 | tf_op jit(solution)/shard_map/all_to_all | solution.py:763
  369.5 108.9 %reduce-scatter.5.cloned.1.call-start = ((), (), s32[]{:S(2)}) async-start(), calls=%async_computation.9 | async-start | bytes 2805760 | tf_op jit(solution)/shard_map/reduce_scatter | solution.py:781
  372.7 209.0 %all-reduce.4.cloned.1.call-start = ((), (), s32[]{:S(2)}) async-start(), calls=%async_computation.10 | async-start | bytes 4399104 | tf_op jit(solution)/shard_map/psum | solution.py:782
  384.0 39.1 %copy-start.10 = (bf16[2048,1024]{1,0:T(8,128)(2,1)S(1)}, bf16[2048,1024]{1,0:T(8,128)(2,1)}, u32[]{:S(2)}) copy-start(bf16[2048,1024]{1,0:T(8,128)(2,1)} %all-gather.3.cloned.1.call-done) | copy-start | bytes 12582916
  384.0 39.1 %copy-start.23 = (f32[2048]{0:T(1024)S(1)}, f32[2048]{0:T(1024)}, u32[]{:S(2)}) copy-start(f32[2048]{0:T(1024)} %copy-done.22) | copy-start | bytes 24580
  384.0 39.1 %copy-start.34 = (f32[2048]{0:T(1024)S(1)}, f32[2048]{0:T(1024)}, u32[]{:S(2)}) copy-start(f32[2048]{0:T(1024)} %copy-done.33) | copy-start | bytes 24580
  423.1 7.4 %copy-start.36 = (f32[1024]{0:T(1024)S(1)}, f32[1024]{0:T(1024)}, u32[]{:S(2)}) copy-start(f32[1024]{0:T(1024)} %copy-done.35) | copy-start | bytes 12292
  423.1 7.4 %copy-start.43 = (bf16[2048,768]{1,0:T(8,128)(2,1)S(1)}, bf16[2048,768]{1,0:T(8,128)(2,1)}, u32[]{:S(2)}) copy-start(bf16[2048,768]{1,0:T(8,128)(2,1)} %attend_back.1) | copy-start | bytes 9437188
  478.4 149.3 %reduce-scatter.3.cloned.1.call-start = ((), (), s32[]{:S(2)}) async-start(), calls=%async_computation.8 | async-start | bytes 5242880 | tf_op jit(solution)/shard_map/reduce_scatter | solution.py:788
  478.4 1.2 copy-start.8
  581.6 3.6 copy-start.11
  627.7 2.1 copy-start.17
  (4 other events, 3.2 us)
Sparse Core Ops, SparseCore 0:
  9.6 51.2 all-gather.2
  62.4 23.6 all-gather.4
  373.5 36.7 reduce-scatter.4
  478.5 103.0 all-reduce.3
  584.0 43.6 reduce-scatter.2
